TPU v7x, 256 devices: a whole 4x4x8 slice. The times are simulated.
256 devices in a mesh: span: 64 (over y_hi, x, z), rows: 4 (over y_lo, core).
Axes of the slice: x: 4, y: 4 (y_hi: 2, y_lo: 2; y = y_hi * 2 + y_lo), z: 8, core: 2. Of those that a mesh axis runs over, the one named last changes fastest.
Arguments:
- pressure_source: float32 [256, 128, 1024], P('span', 'rows'), may hold values from -6 to 6
- geometry: float32 [64, 3, 128, 1024], P('span', None, 'rows'), may hold values from 0.1 to 1
- owner: int32 [1], replicated, may hold values from 0 to 63
Outputs:
- pressure: float32 [256, 128, 1024], P('span', 'rows')
Inputs may be any that keep to these rules, and one draw needn't show every extreme that they name: owner is a span index.
All inputs are finite; a program needn't handle non-finite values.
Results may differ from a plain program's by a relative error of at most 0.00011.
Values sent between devices are 32-bit elements; how exact they have to be, the bound alone decides.
A program may use at most 64 MiB of HBM per device.

v0:
```python
import math
import jax
import jax.numpy as jnp
from jax import lax
from jax.sharding import Mesh
from jax.sharding import PartitionSpec as P

SWEEPS = 2
STEPS = 8
SPAN = ("span_0", "span_1", "span_2")
ROWS = ("rows_0", "rows_1")
LOWER_BOUND = 0.02
UPPER_BOUND = 2.0
HIGHEST = lax.Precision.HIGHEST


def spread(x, axes, root):
    x = jnp.where(lax.axis_index(axes) == root, x, jnp.zeros_like(x))
    for axis in axes:
        x = lax.psum(x, axis)
    return x


def in_one_piece(arrays, axis, split_dim, concat_dim, along):
    ends, at = ([], 0)
    for a in arrays[:-1]:
        at += a.shape[along]
        ends.append(at)
    both = jnp.concatenate(arrays, axis=along)
    return tuple(
        jnp.split(
            lax.all_to_all(both, axis, split_axis=split_dim, concat_axis=concat_dim, tiled=True),
            ends,
            axis=along,
        )
    )


def in_blocks(x, dim, size):
    before, after = (x.shape[:dim], x.shape[dim + 1 :])
    return jnp.moveaxis(x.reshape(*before, size, -1, *after), dim, 0)


def laid_out(parts, dim):
    dims = list(parts.shape[1:])
    dims[dim] *= parts.shape[0]
    return jnp.moveaxis(parts, 0, dim).reshape(dims)


def moved_by_axis(parts, axes, order):
    dims = [lax.axis_size(a) for a in axes]
    parts = parts.reshape(*dims, *parts.shape[1:])
    for k in order:
        parts = lax.all_to_all(parts, axes[k], split_axis=k, concat_axis=k, tiled=True)
    return parts.reshape(-1, *parts.shape[len(axes) :])


def core_and_chips(x, groups, order, split_dim, concat_dim):
    size = lax.axis_size(groups[0]) * lax.axis_size(groups[1])
    parts = in_blocks(x, split_dim, size)
    return laid_out(moved_by_axis(parts, groups, order), concat_dim)


def side_by_side(arrays, axis, dim, along):
    ends, at = ([], 0)
    for a in arrays[:-1]:
        at += a.shape[along]
        ends.append(at)
    both = jnp.concatenate(arrays, axis=along)
    return tuple(jnp.split(lax.all_gather(both, axis, axis=dim, tiled=True), ends, axis=along))


def reverse_bits(number, bit_count):
    result = number * 0
    for level in range(bit_count):
        result = result + number // 2**level % 2 * 2 ** (bit_count - 1 - level)
    return result


def apply_faces(planes, upper_rows, lower_rows, coeffs):
    left_face, right_face, top_face, bottom_face, diagonal = coeffs
    zero_col = jnp.zeros_like(planes[:, :, :1])
    left_cols = jnp.concatenate([zero_col, planes[:, :, :-1]], axis=2)
    right_cols = jnp.concatenate([planes[:, :, 1:], zero_col], axis=2)
    return (
        diagonal * planes
        - left_face * left_cols
        - right_face * right_cols
        - top_face * upper_rows
        - bottom_face * lower_rows
    )


def plain_operator(planes, coeffs):
    zero_row = jnp.zeros_like(planes[:, :1])
    upper_rows = jnp.concatenate([zero_row, planes[:, :-1]], axis=1)
    lower_rows = jnp.concatenate([planes[:, 1:], zero_row], axis=1)
    return apply_faces(planes, upper_rows, lower_rows, coeffs)


def chebyshev(rhs, coeffs, operator):
    center = (UPPER_BOUND + LOWER_BOUND) / 2.0
    half_width = (UPPER_BOUND - LOWER_BOUND) / 2.0
    sigma_ratio = center / half_width
    inverse_diag = 1.0 / coeffs[4]
    solution = jnp.zeros_like(rhs)
    residual = rhs
    for sweep_index in range(SWEEPS):
        ratio_now = 1.0 / sigma_ratio
        direction = residual * inverse_diag / center
        for step_index in range(STEPS):
            solution = solution + direction
            residual = residual - operator(direction, coeffs)
            ratio_next = 1.0 / (2.0 * sigma_ratio - ratio_now)
            direction = (
                ratio_next * ratio_now * direction
                + 2.0 * ratio_next / half_width * residual * inverse_diag
            )
            ratio_now = ratio_next
    return solution


def on_device(pressure_source, geometry, owner):
    span_count = lax.axis_size(SPAN)
    device = lax.axis_index(SPAN)
    bit_count = span_count.bit_length() - 1
    local_count, row_count, col_count = pressure_source.shape
    total_len = local_count * span_count
    plane = spread(geometry[0], SPAN, owner[0])
    west_face = plane[0]
    north_face = plane[1]
    volume = plane[2]
    merged = pressure_source.reshape((1, local_count * row_count, col_count))
    received = lax.all_to_all(merged, SPAN, split_axis=1, concat_axis=0, tiled=True)
    positions = jnp.arange(span_count, dtype=jnp.int32)
    freqs = reverse_bits(positions, bit_count)
    phase = (freqs[:, None] * positions[None, :] % span_count).astype(jnp.float32) * (
        -2.0 * math.pi / span_count
    )
    real_rows = jnp.einsum("rd,dtc->rtc", jnp.cos(phase), received, precision=HIGHEST)
    imag_rows = jnp.einsum("rd,dtc->rtc", jnp.sin(phase), received, precision=HIGHEST)
    real_back, imag_back = in_one_piece((real_rows, imag_rows), SPAN, 0, 1, 2)
    real_part = real_back.reshape(pressure_source.shape)
    imag_part = imag_back.reshape(pressure_source.shape)
    frequency = reverse_bits(device, bit_count)
    local_index = jnp.arange(local_count, dtype=jnp.int32)
    mode_index = frequency + span_count * local_index
    forward_phase = (mode_index[:, None] * local_index[None, :] % total_len).astype(jnp.float32) * (
        -2.0 * math.pi / total_len
    )
    forward_cos = jnp.cos(forward_phase)
    forward_sin = jnp.sin(forward_phase)
    spec_real = jnp.einsum("kj,jyc->kyc", forward_cos, real_part, precision=HIGHEST) - jnp.einsum(
        "kj,jyc->kyc", forward_sin, imag_part, precision=HIGHEST
    )
    spec_imag = jnp.einsum("kj,jyc->kyc", forward_sin, real_part, precision=HIGHEST) + jnp.einsum(
        "kj,jyc->kyc", forward_cos, imag_part, precision=HIGHEST
    )
    eigen = 2.0 - 2.0 * jnp.cos(mode_index.astype(jnp.float32) * (2.0 * math.pi / total_len))
    eigen_both = jnp.concatenate([eigen, eigen], axis=0)
    stacked = jnp.concatenate([spec_real, spec_imag], axis=0)
    rows_count = lax.axis_size(ROWS)
    row_device = lax.axis_index(ROWS)
    per_device = 2 * local_count // rows_count
    mine = core_and_chips(stacked, ("rows_0", "rows_1"), (1, 0), 0, 1)
    west_all, north_all, volume_all = side_by_side((west_face, north_face, volume), ROWS, 0, 1)
    east_all = jnp.concatenate([west_all[:, 1:], jnp.zeros_like(west_all[:, :1])], axis=1)
    south_all = jnp.concatenate([north_all[1:], jnp.zeros_like(north_all[:1])], axis=0)
    face_total = west_all + east_all + north_all + south_all
    eigen_mine = lax.dynamic_slice_in_dim(eigen_both, row_device * per_device, per_device)
    diagonal = face_total[None] + eigen_mine[:, None, None] * volume_all[None]
    coeffs = (west_all, east_all, north_all, south_all, diagonal)
    solved_mine = chebyshev(mine, coeffs, plain_operator)
    solved = lax.all_to_all(solved_mine, ROWS, split_axis=1, concat_axis=0, tiled=True)
    solved_real = solved[:local_count]
    solved_imag = solved[local_count:]
    inverse_cos = jnp.transpose(forward_cos) / local_count
    inverse_sin = -jnp.transpose(forward_sin) / local_count
    real_part = jnp.einsum("jk,kyc->jyc", inverse_cos, solved_real, precision=HIGHEST) - jnp.einsum(
        "jk,kyc->jyc", inverse_sin, solved_imag, precision=HIGHEST
    )
    imag_part = jnp.einsum("jk,kyc->jyc", inverse_sin, solved_real, precision=HIGHEST) + jnp.einsum(
        "jk,kyc->jyc", inverse_cos, solved_imag, precision=HIGHEST
    )
    merged_real = real_part.reshape((1, local_count * row_count, col_count))
    merged_imag = imag_part.reshape((1, local_count * row_count, col_count))
    recv_real, recv_imag = in_one_piece((merged_real, merged_imag), SPAN, 1, 0, 2)
    positions = jnp.arange(span_count, dtype=jnp.int32)
    freqs = reverse_bits(positions, bit_count)
    phase = (positions[:, None] * freqs[None, :] % span_count).astype(jnp.float32) * (
        2.0 * math.pi / span_count
    )
    gathered_rows = (
        jnp.einsum("ds,stc->dtc", jnp.cos(phase), recv_real, precision=HIGHEST)
        - jnp.einsum("ds,stc->dtc", jnp.sin(phase), recv_imag, precision=HIGHEST)
    ) / span_count
    pressure_back = lax.all_to_all(gathered_rows, SPAN, split_axis=0, concat_axis=1, tiled=True)
    return pressure_back.reshape(pressure_source.shape)


def solution(mesh):
    torus = Mesh(
        mesh.devices.reshape(2, 4, 8, 2, 2), ("span_0", "span_1", "span_2", "rows_0", "rows_1")
    )
    in_specs = (P(SPAN, ROWS, None), P(SPAN, None, ROWS, None), P())
    out_specs = P(SPAN, ROWS, None)
    return jax.shard_map(
        on_device, mesh=torus, in_specs=in_specs, out_specs=out_specs, check_vma=False
    )
```

profile of v0, /device:TPU:6, one launch (start us, length us, event | category | flops | bytes accessed | tf_op | source)
XLA Modules:
  0.0 380.6 jit_solution(5118960952709081886)
XLA Ops:
  6.5 2.5 reshape.288
  9.0 14.6 %all-to-all-start = ((f32[1,128,1024]{2,0,1:T(1,128)}), f32[1,128,1024]{2,0,1:T(1,128)S(1)}, u32[]{:S(2)}, u32[]{:S(2)}) async-start(f32[1,128,1024]{2,0,1:T(1,128)} %reshape.288), calls=%async_computation | async-start | bytes 1048576 | tf_op jit(solution)/shard_map/all_to_all | solution.py:134
  25.3 41.9 %all-reduce.66.cloned.1.call-done = f32[3,32,1024]{2,1,0:T(8,128)} async-done(((f32[3,32,1024]{2,1,0:T(8,128)}), f32[3,32,1024]{2,1,0:T(8,128)}) %all-reduce.66.cloned.1.call-update) | async-done | bytes 393232 | tf_op jit(solution)/shard_map/psum | solution.py:20
  67.2 1.2 reduce
  70.7 1.8 copy.21
  72.4 10.6 %all-to-all-start.1 = ((f32[64,2,2048]{2,1,0:T(2,128)}), f32[64,2,2048]{2,1,0:T(2,128)S(1)}, u32[]{:S(2)}, u32[]{:S(2)}) async-start(f32[64,2,2048]{2,1,0:T(2,128)} %copy.21), calls=%async_computation.1 | async-start | bytes 2097152 | tf_op jit(solution)/shard_map/all_to_all | solution.py:32
  83.1 35.4 %all-reduce.68.cloned.1.call-done = f32[3,32,1024]{2,1,0:T(8,128)} async-done(((f32[3,32,1024]{2,1,0:T(8,128)}), f32[3,32,1024]{2,1,0:T(8,128)}) %all-reduce.68.cloned.1.call-update) | async-done | bytes 393232 | tf_op jit(solution)/shard_map/psum | solution.py:20
  118.7 76.7 %all-reduce.70.cloned.1.call-done = f32[3,32,1024]{2,1,0:T(8,128)} async-done(((f32[3,32,1024]{2,1,0:T(8,128)}), f32[3,32,1024]{2,1,0:T(8,128)}) %all-reduce.70.cloned.1.call-update) | async-done | bytes 393232 | tf_op jit(solution)/shard_map/psum | solution.py:20
  195.4 1.1 slice_bitcast_fusion.2
  198.3 1.3 fusion.11
  199.6 1.3 fusion.13
  200.9 1.3 convolution_subtract_fusion.1
  202.2 1.3 convolution_add_fusion.1
  204.6 4.6 %all_to_all.70 = f32[2,2,2,32,1024]{4,2,0,3,1:T(2,128)S(1)} all-to-all(f32[2,2,2,32,1024]{4,2,0,3,1:T(2,128)S(1)} %copy.26), channel_id=1, replica_groups=mesh['span_0'=2,'span_1'=4,'span_2'=8,'rows_0'=2,'rows_1'=2] {'rows_1'}, dimensions={1} | all-to-all | bytes 2097152 | tf_op jit(solution)/shard_map/all_to_all | solution.py:54
  209.1 1.1 copy.27
  210.3 4.4 %all-to-all-start.3 = ((f32[2,2,2,32,1024]{4,2,1,3,0:T(2,128)}), f32[2,2,2,32,1024]{4,2,1,3,0:T(2,128)}, u32[]{:S(2)}, u32[]{:S(2)}) async-start(f32[2,2,2,32,1024]{4,2,1,3,0:T(2,128)} %copy.27), calls=%async_computation.3 | async-start | bytes 2097152 | tf_op jit(solution)/shard_map/all_to_all | solution.py:54
  214.9 13.3 %all-gather.2.cloned.1.call-done = f32[128,3072]{1,0:T(8,128)} async-done(((f32[32,3072]{1,0:T(8,128)}), f32[128,3072]{1,0:T(8,128)}) %all-gather.2.cloned.1.call-update) | async-done | bytes 1572880 | tf_op jit(solution)/shard_map/all_gather | solution.py:70
  228.2 1.2 slice.282
  229.4 1.3 slice.281
  231.0 3.6 all-to-all-done.3
  234.7 1.8 copy.28
  237.4 1.0 multiply_add_fusion.12
  239.1 2.1 multiply_add_fusion.11
  241.9 1.2 multiply_add_fusion.10
  243.7 1.2 multiply_add_fusion.9
  245.4 1.2 multiply_add_fusion.8
  247.2 1.2 multiply_add_fusion.7
  248.9 1.2 multiply_add_fusion.6
  250.7 1.2 broadcast_multiply_fusion
  252.5 1.1 multiply_add_fusion.5
  253.6 1.7 fusion.150
  255.3 1.9 fusion.151
  257.2 3.5 multiply_add_fusion.4
  261.4 1.2 multiply_add_fusion.3
  263.1 1.2 multiply_add_fusion.2
  264.9 1.2 multiply_add_fusion.1
  266.7 1.2 multiply_add_fusion
  268.3 1.2 fusion.141
  269.5 4.6 %add_add_fusion = f32[2,128,1024]{2,1,0:T(8,128)S(1)} fusion(f32[2,127,1024]{2,1,0:T(8,128)} %get-tuple-element.38, f32[2,127,1024]{2,1,0:T(8,128)S(1)} %get-tuple-element.37, f32[2,128,1023]{2,1,0:T(8,128)S(1)} %get-tuple-element.36, f32[2,128,1023]{2,1,0:T(8,128)S(1)} %get-tuple-element.35, f32[2,128,1024]{2,1,0:T(8,128)S(1)} %get-tuple-element.7, ...), kind=kLoop, calls=%fused_computation.11 | loop fusion | flops 15204352 | bytes 27226120 | tf_op jit(solution)/shard_map/add | solution.py:112
  275.0 17.0 %all_to_all.71 = f32[2,128,1024]{2,0,1:T(2,128)S(1)} all-to-all(f32[2,128,1024]{2,0,1:T(2,128)S(1)} %copy.29), channel_id=1, replica_groups=mesh['span_0'=2,'span_1'=4,'span_2'=8,'rows_0'=2,'rows_1'=2] {'rows_0','..., dimensions={1} | all-to-all | bytes 2097152 | tf_op jit(solution)/shard_map/all_to_all | solution.py:174
  294.4 1.0 fusion.53
  296.3 1.0 convolution_subtract_fusion
  297.3 1.0 convolution_add_fusion
  299.1 1.1 copy.35
  300.2 43.1 %all_to_all.72 = f32[1,128,2048]{2,0,1:T(1,128)S(1)} all-to-all(f32[1,128,2048]{2,0,1:T(1,128)S(1)} %copy.35), channel_id=1, replica_groups=mesh['span_0'=2,'span_1'=4,'span_2'=8,'rows_0'=2,'rows_1'=2] {'span_0','..., dimensions={1} | all-to-all | bytes 2097152 | tf_op jit(solution)/shard_map/all_to_all | solution.py:32
  343.2 2.5 reduce.1
  348.5 24.2 %all_to_all.73 = f32[64,2,1024]{2,1,0:T(2,128)S(1)} all-to-all(f32[64,2,1024]{2,1,0:T(2,128)S(1)} %copy.38), channel_id=1, replica_groups=mesh['span_0'=2,'span_1'=4,'span_2'=8,'rows_0'=2,'rows_1'=2] {'span_0','..., dimensions={0} | all-to-all | bytes 1048576 | tf_op jit(solution)/shard_map/all_to_all | solution.py:197
  372.7 1.2 reshape.295
  (75 shorter events, 22.3 us)
Async XLA Ops:
  6.5 17.9 %copy-start.1 = (f32[1,3,32,1024]{3,2,1,0:T(8,128)S(1)}, f32[1,3,32,1024]{3,2,1,0:T(8,128)}, u32[]{:S(2)}) copy-start(f32[1,3,32,1024]{3,2,1,0:T(8,128)} %param.4) | copy-start | bytes 1179652
  9.0 58.2 %all-to-all-start = ((f32[1,128,1024]{2,0,1:T(1,128)}), f32[1,128,1024]{2,0,1:T(1,128)S(1)}, u32[]{:S(2)}, u32[]{:S(2)}) async-start(f32[1,128,1024]{2,0,1:T(1,128)} %reshape.288), calls=%async_computation | async-start | bytes 1048576 | tf_op jit(solution)/shard_map/all_to_all | solution.py:134
  23.7 43.5 %all-reduce.66.cloned.1.call-start = ((), (), s32[]{:S(2)}) async-start(), calls=%async_computation.7 | async-start | bytes 786432 | tf_op jit(solution)/shard_map/psum | solution.py:20
  25.2 93.2 %all-reduce.68.cloned.1.call-start = ((), (), s32[]{:S(2)}) async-start(), calls=%async_computation.8 | async-start | bytes 786432 | tf_op jit(solution)/shard_map/psum | solution.py:20
  72.4 125.0 %all-to-all-start.1 = ((f32[64,2,2048]{2,1,0:T(2,128)}), f32[64,2,2048]{2,1,0:T(2,128)S(1)}, u32[]{:S(2)}, u32[]{:S(2)}) async-start(f32[64,2,2048]{2,1,0:T(2,128)} %copy.21), calls=%async_computation.1 | async-start | bytes 2097152 | tf_op jit(solution)/shard_map/all_to_all | solution.py:32
  83.0 112.4 %all-reduce.70.cloned.1.call-start = ((), (), s32[]{:S(2)}) async-start(), calls=%async_computation.9 | async-start | bytes 786432 | tf_op jit(solution)/shard_map/psum | solution.py:20
  118.5 109.7 %all-gather.2.cloned.1.call-start = ((), (), s32[]{:S(2)}) async-start(), calls=%async_computation.10 | async-start | bytes 1966080 | tf_op jit(solution)/shard_map/all_gather | solution.py:70
  210.3 24.4 %all-to-all-start.3 = ((f32[2,2,2,32,1024]{4,2,1,3,0:T(2,128)}), f32[2,2,2,32,1024]{4,2,1,3,0:T(2,128)}, u32[]{:S(2)}, u32[]{:S(2)}) async-start(f32[2,2,2,32,1024]{4,2,1,3,0:T(2,128)} %copy.27), calls=%async_computation.3 | async-start | bytes 2097152 | tf_op jit(solution)/shard_map/all_to_all | solution.py:54
  228.2 2.5 copy-start
Sparse Core Ops, SparseCore 0:
  27.1 40.0 all-reduce.65
  69.6 48.7 all-reduce.67
  120.8 74.6 all-reduce.69
  197.4 30.7 all-gather.1
where the time goes:
time: 387 us; the launch traced here: 381 us
  waiting for transfers between devices  171 us (44%)
  blocking collectives  88.9 us (23%)
  local copies, waits for them, and re-layouts  32.6 us (8%)
  other arithmetic  30.6 us (8%)
  starting transfers between devices  30 us (8%)
  between operations  14.8 us (4%)
  matrix products  12.8 us (3%)
    psum x3, waiting for transfers between devices, spread(): x = lax.psum(x, axis)  154 us
    all_to_all x1, blocking collectives, in_one_piece(): lax.all_to_all(both, axis, split_axis=split_dim, concat_axis=concat_dim,...  43.1 us
    all_to_all x1, blocking collectives, on_device(): lax.all_to_all(gathered_rows, SPAN, split_axis=0, concat_axis=1, tiled=True)  24.2 us
    add x13, other arithmetic, chebyshev(): ratio_next * ratio_now * direction  18.3 us
    all_to_all x1, blocking collectives, on_device(): lax.all_to_all(solved_mine, ROWS, split_axis=1, concat_axis=0, tiled=True)  17 us
    all_to_all x1, starting transfers between devices, on_device(): lax.all_to_all(merged, SPAN, split_axis=1, concat_axis=0, tiled=True)  14.6 us
    all_gather x1, waiting for transfers between devices, side_by_side(): lax.all_gather(both, axis, axis=dim, tiled=True)  13.3 us
    all_to_all x1, starting transfers between devices, in_one_piece(): lax.all_to_all(both, axis, split_axis=split_dim, concat_axis=concat_dim,...  10.6 us
  transfers between devices with their start and end apart: 7, of which 5 were waited for; matrix products, arithmetic and copies ran while one was open for 5% of the time, Pallas kernels for 0%

commit v1 on v0

--- a/solution.py
+++ b/solution.py
@@ -17,7 +17,8 @@
 def spread(x, axes, root):
     x = jnp.where(lax.axis_index(axes) == root, x, jnp.zeros_like(x))
     for axis in axes:
-        x = lax.psum(x, axis)
+        shaped = lax.all_gather(x, axis)
+        x = jnp.sum(shaped, axis=0)
     return x
 
 

time: 387 us -> 323 us (0.83)
  waiting for transfers between devices: 171 us -> 100 us
  blocking collectives: 88.9 us -> 101 us
  starting transfers between devices: 30 us -> 22.5 us
  other arithmetic: 30.6 us -> 36 us
    psum x3 -> x0, waiting for transfers between devices: 154 us -> none  [spread(): x = lax.psum(x, axis)]
    all_gather x0 -> x2, waiting for transfers between devices: none -> 51.9 us  [spread(): shaped = lax.all_gather(x, axis)]
    all_to_all x1, waiting for transfers between devices: 0.01 us -> 25.3 us  [on_device(): lax.all_to_all(merged, SPAN, split_axis=1, concat_axis=0, tiled=True)]
    all_gather x1, waiting for transfers between devices: 13.3 us -> 0.02 us  [side_by_side(): lax.all_gather(both, axis, axis=dim, tiled=True)]
    all_gather x0 -> x1, blocking collectives: none -> 13 us  [spread(): shaped = lax.all_gather(x, axis)]
    all_to_all x1, waiting for transfers between devices: 3.65 us -> 14 us  [moved_by_axis(): lax.all_to_all(parts, axes[k], split_axis=k, concat_axis=k, tiled=True)]
    all_to_all x1, waiting for transfers between devices: 0.01 us -> 8.95 us  [in_one_piece(): lax.all_to_all(both, axis, split_axis=split_dim, concat_axis=concat_dim,...]
    reduce_sum x0 -> x3, other arithmetic: none -> 5.26 us  [spread(): x = jnp.sum(shaped, axis=0)]
  transfers between devices with their start and end apart: 7 -> 6, of which waited for: 5 -> 5; matrix products, arithmetic and copies ran while one was open for 5% -> 6% of each run, Pallas kernels for 0% -> 0%
where the time goes in v1:
time: 323 us; the launch traced here: 316 us
  blocking collectives  101 us (31%)
  waiting for transfers between devices  100 us (31%)
  other arithmetic  36 us (11%)
  local copies, waits for them, and re-layouts  29.4 us (9%)
  starting transfers between devices  22.5 us (7%)
  between operations  14.8 us (5%)
  matrix products  12.8 us (4%)
    all_gather x2, waiting for transfers between devices, spread(): shaped = lax.all_gather(x, axis)  51.9 us
    all_to_all x1, blocking collectives, in_one_piece(): lax.all_to_all(both, axis, split_axis=split_dim, concat_axis=concat_dim,...  41.7 us
    all_to_all x1, waiting for transfers between devices, on_device(): lax.all_to_all(merged, SPAN, split_axis=1, concat_axis=0, tiled=True)  25.3 us
    all_to_all x1, blocking collectives, on_device(): lax.all_to_all(gathered_rows, SPAN, split_axis=0, concat_axis=1, tiled=True)  24.2 us
    add x13, other arithmetic, chebyshev(): ratio_next * ratio_now * direction  18.9 us
    all_to_all x1, blocking collectives, on_device(): lax.all_to_all(solved_mine, ROWS, split_axis=1, concat_axis=0, tiled=True)  17 us
    all_to_all x1, waiting for transfers between devices, moved_by_axis(): lax.all_to_all(parts, axes[k], split_axis=k, concat_axis=k, tiled=True)  14 us
    all_gather x1, blocking collectives, spread(): shaped = lax.all_gather(x, axis)  13 us
  transfers between devices with their start and end apart: 6, of which 5 were waited for; matrix products, arithmetic and copies ran while one was open for 6% of the time, Pallas kernels for 0%

profile of v1, /device:TPU:6, one launch (start us, length us, event | category | flops | bytes accessed | tf_op | source)
XLA Modules:
  0.0 316.3 jit_solution(6916310463067786564)
XLA Ops:
  7.2 13.0 %all_gather.19 = f32[2,3,32,1024]{3,2,1,0:T(8,128)S(1)} all-gather(f32[1,3,32,1024]{3,2,1,0:T(8,128)S(1)} %broadcast_select_fusion), channel_id=1, replica_groups=mesh['span_0'=2,'span_1'=4,'span_2'=8,'rows_0'=2,'rows_1'=2] {'span_0'}, dimensions={0}, use_global_device_ids=true | all-gather | bytes 1179648 | tf_op jit(solution)/shard_map/all_gather | solution.py:20
  21.1 31.0 %all-gather.8.cloned.1.call-done = f32[12,32,1024]{2,1,0:T(8,128)} async-done(((f32[3,32,1024]{2,1,0:T(8,128)}), f32[12,32,1024]{2,1,0:T(8,128)}) %all-gather.8.cloned.1.call-update) | async-done | bytes 1572880 | tf_op jit(solution)/shard_map/all_gather | solution.py:20
  52.2 2.3 reduce_sum.28
  54.5 1.4 reshape.285
  55.9 12.9 %all-to-all-start = ((f32[1,128,1024]{2,0,1:T(1,128)}), f32[1,128,1024]{2,0,1:T(1,128)S(1)}, u32[]{:S(2)}, u32[]{:S(2)}) async-start(f32[1,128,1024]{2,0,1:T(1,128)} %reshape.285), calls=%async_computation | async-start | bytes 1048576 | tf_op jit(solution)/shard_map/all_to_all | solution.py:135
  68.8 25.3 %all-to-all-done = f32[1,128,1024]{2,0,1:T(1,128)S(1)} async-done(((f32[1,128,1024]{2,0,1:T(1,128)}), f32[1,128,1024]{2,0,1:T(1,128)S(1)}, u32[]{:S(2)}, u32[]{:S(2)}) %all-to-all-start) | async-done | bytes 524320 | tf_op jit(solution)/shard_map/all_to_all | solution.py:135
  94.2 1.2 reduce
  97.6 1.8 copy.21
  99.4 5.8 %all-to-all-start.1 = ((f32[64,2,2048]{2,1,0:T(2,128)}), f32[64,2,2048]{2,1,0:T(2,128)S(1)}, u32[]{:S(2)}, u32[]{:S(2)}) async-start(f32[64,2,2048]{2,1,0:T(2,128)} %copy.21), calls=%async_computation.1 | async-start | bytes 2097152 | tf_op jit(solution)/shard_map/all_to_all | solution.py:33
  105.4 20.9 %all-gather.10.cloned.1.call-done = f32[24,32,1024]{2,1,0:T(8,128)} async-done(((f32[3,32,1024]{2,1,0:T(8,128)}), f32[24,32,1024]{2,1,0:T(8,128)}) %all-gather.10.cloned.1.call-update) | async-done | bytes 3145744 | tf_op jit(solution)/shard_map/all_gather | solution.py:20
  126.3 2.2 reduce_sum.29
  129.4 8.9 %all-to-all-done.1 = f32[64,2,2048]{2,1,0:T(2,128)S(1)} async-done(((f32[64,2,2048]{2,1,0:T(2,128)}), f32[64,2,2048]{2,1,0:T(2,128)S(1)}, u32[]{:S(2)}, u32[]{:S(2)}) %all-to-all-start.1) | async-done | bytes 1048608 | tf_op jit(solution)/shard_map/all_to_all | solution.py:33
  139.2 1.3 fusion.11
  140.5 1.3 fusion.13
  141.8 1.3 convolution_subtract_fusion.1
  143.2 1.3 convolution_add_fusion.1
  145.5 4.6 %all_to_all.70 = f32[2,2,2,32,1024]{4,2,0,3,1:T(2,128)S(1)} all-to-all(f32[2,2,2,32,1024]{4,2,0,3,1:T(2,128)S(1)} %copy.26), channel_id=1, replica_groups=mesh['span_0'=2,'span_1'=4,'span_2'=8,'rows_0'=2,'rows_1'=2] {'rows_1'}, dimensions={1} | all-to-all | bytes 2097152 | tf_op jit(solution)/shard_map/all_to_all | solution.py:55
  150.1 1.1 copy.27
  151.2 3.6 %all-to-all-start.3 = ((f32[2,2,2,32,1024]{4,2,1,3,0:T(2,128)}), f32[2,2,2,32,1024]{4,2,1,3,0:T(2,128)S(1)}, u32[]{:S(2)}, u32[]{:S(2)}) async-start(f32[2,2,2,32,1024]{4,2,1,3,0:T(2,128)} %copy.27), calls=%async_computation.3 | async-start | bytes 2097152 | tf_op jit(solution)/shard_map/all_to_all | solution.py:55
  155.0 14.0 %all-to-all-done.3 = f32[2,2,2,32,1024]{4,2,1,3,0:T(2,128)S(1)} async-done(((f32[2,2,2,32,1024]{4,2,1,3,0:T(2,128)}), f32[2,2,2,32,1024]{4,2,1,3,0:T(2,128)S(1)}, u32[]{:S(2)}, u32[]{:S(2)}) %all-to-all-start.3) | async-done | bytes 1048608 | tf_op jit(solution)/shard_map/all_to_all | solution.py:55
  169.6 1.2 slice.282
  170.8 1.3 slice.281
  175.2 2.1 multiply_add_fusion.11
  178.0 1.3 multiply_add_fusion.10
  179.9 1.3 multiply_add_fusion.9
  181.9 1.3 multiply_add_fusion.8
  183.8 1.3 multiply_add_fusion.7
  185.8 1.3 multiply_add_fusion.6
  187.7 1.3 broadcast_multiply_fusion
  189.7 1.0 multiply_add_fusion.5
  190.7 1.7 fusion.150
  192.5 1.9 fusion.151
  194.4 3.6 %multiply_add_fusion.4 = (f32[2,128,1024]{2,1,0:T(8,128)S(1)}, f32[2,128,1024]{2,1,0:T(8,128)S(1)}) fusion(f32[2,128,1024]{2,1,0:T(8,128)S(1)} %multiply_add_fusion.5, f32[128,1024]{1,0:T(8,128)S(1)} %get-tuple-element.29, f32[2]{0:T(128)S(1)} %dynamic_slice.3, f32[128,1024]{1,0:T(8,128)S(1)} %get-tuple-element.28, f32[2,127,1024]{2,1,0:T(8,128)} %get-tuple-element.58, ...), kind=kLoop, calls=%fused_computation.20 | loop fusion | flops 7602176 | bytes 15691784 | tf_op jit(solution)/shard_map/add | solution.py:117
  198.5 1.1 multiply_add_fusion.3
  200.3 1.1 multiply_add_fusion.2
  202.0 1.2 multiply_add_fusion.1
  203.7 1.2 multiply_add_fusion
  205.4 1.2 fusion.141
  206.6 4.6 %add_add_fusion = f32[2,128,1024]{2,1,0:T(8,128)S(1)} fusion(f32[2,127,1024]{2,1,0:T(8,128)} %get-tuple-element.38, f32[2,127,1024]{2,1,0:T(8,128)S(1)} %get-tuple-element.37, f32[2,128,1023]{2,1,0:T(8,128)S(1)} %get-tuple-element.36, f32[2,128,1023]{2,1,0:T(8,128)S(1)} %get-tuple-element.35, f32[2,128,1024]{2,1,0:T(8,128)S(1)} %get-tuple-element.7, ...), kind=kLoop, calls=%fused_computation.11 | loop fusion | flops 15204352 | bytes 27226120 | tf_op jit(solution)/shard_map/add | solution.py:113
  212.1 17.0 %all_to_all.71 = f32[2,128,1024]{2,0,1:T(2,128)S(1)} all-to-all(f32[2,128,1024]{2,0,1:T(2,128)S(1)} %copy.29), channel_id=1, replica_groups=mesh['span_0'=2,'span_1'=4,'span_2'=8,'rows_0'=2,'rows_1'=2] {'rows_0','..., dimensions={1} | all-to-all | bytes 2097152 | tf_op jit(solution)/shard_map/all_to_all | solution.py:175
  230.4 1.0 fusion.45
  233.3 1.0 convolution_subtract_fusion
  234.4 1.0 convolution_add_fusion
  236.1 1.1 copy.35
  237.2 41.7 %all_to_all.72 = f32[1,128,2048]{2,0,1:T(1,128)S(1)} all-to-all(f32[1,128,2048]{2,0,1:T(1,128)S(1)} %copy.35), channel_id=1, replica_groups=mesh['span_0'=2,'span_1'=4,'span_2'=8,'rows_0'=2,'rows_1'=2] {'span_0','..., dimensions={1} | all-to-all | bytes 2097152 | tf_op jit(solution)/shard_map/all_to_all | solution.py:33
  278.9 2.5 reduce.1
  284.2 24.2 %all_to_all.73 = f32[64,2,1024]{2,1,0:T(2,128)S(1)} all-to-all(f32[64,2,1024]{2,1,0:T(2,128)S(1)} %copy.38), channel_id=1, replica_groups=mesh['span_0'=2,'span_1'=4,'span_2'=8,'rows_0'=2,'rows_1'=2] {'span_0','..., dimensions={0} | all-to-all | bytes 1048576 | tf_op jit(solution)/shard_map/all_to_all | solution.py:198
  308.4 1.2 reshape.292
  (76 shorter events, 24.2 us)
Async XLA Ops:
  6.5 45.6 %all-gather.8.cloned.1.call-start = ((), (), s32[]{:S(2)}) async-start(), calls=%async_computation.8 | async-start | bytes 1966080 | tf_op jit(solution)/shard_map/all_gather | solution.py:20
  21.1 33.4 %copy-start.1 = (f32[4,32,1024]{2,1,0:T(8,128)S(1)}, f32[4,32,1024]{2,1,0:T(8,128)}, u32[]{:S(2)}) copy-start(f32[4,32,1024]{2,1,0:T(8,128)} %param.3) | copy-start | bytes 1572868
  21.1 105.2 %all-gather.10.cloned.1.call-start = ((), (), s32[]{:S(2)}) async-start(), calls=%async_computation.9 | async-start | bytes 3538944 | tf_op jit(solution)/shard_map/all_gather | solution.py:20
  55.9 38.3 %all-to-all-start = ((f32[1,128,1024]{2,0,1:T(1,128)}), f32[1,128,1024]{2,0,1:T(1,128)S(1)}, u32[]{:S(2)}, u32[]{:S(2)}) async-start(f32[1,128,1024]{2,0,1:T(1,128)} %reshape.285), calls=%async_computation | async-start | bytes 1048576 | tf_op jit(solution)/shard_map/all_to_all | solution.py:135
  99.4 39.0 %all-to-all-start.1 = ((f32[64,2,2048]{2,1,0:T(2,128)}), f32[64,2,2048]{2,1,0:T(2,128)S(1)}, u32[]{:S(2)}, u32[]{:S(2)}) async-start(f32[64,2,2048]{2,1,0:T(2,128)} %copy.21), calls=%async_computation.1 | async-start | bytes 2097152 | tf_op jit(solution)/shard_map/all_to_all | solution.py:33
  105.2 64.4 %all-gather.6.cloned.1.call-start = ((), (), s32[]{:S(2)}) async-start(), calls=%async_computation.7 | async-start | bytes 1966080 | tf_op jit(solution)/shard_map/all_gather | solution.py:71
  151.2 17.8 %all-to-all-start.3 = ((f32[2,2,2,32,1024]{4,2,1,3,0:T(2,128)}), f32[2,2,2,32,1024]{4,2,1,3,0:T(2,128)S(1)}, u32[]{:S(2)}, u32[]{:S(2)}) async-start(f32[2,2,2,32,1024]{4,2,1,3,0:T(2,128)} %copy.27), calls=%async_computation.3 | async-start | bytes 2097152 | tf_op jit(solution)/shard_map/all_to_all | solution.py:55
  169.6 2.5 copy-start
Sparse Core Ops, SparseCore 0:
  21.2 30.8 all-gather.7
  54.6 71.6 all-gather.9
  129.4 26.9 all-gather.5
